TPU v7x, 256 devices: a whole 4x4x8 slice. The times are simulated.
256 devices in a mesh: cp: 8 (over x, z_hi), fsdp: 32 (over z_lo, y, core).
Axes of the slice: x: 4, y: 4, z: 8 (z_hi: 2, z_lo: 4; z = z_hi * 4 + z_lo), core: 2. Of those that a mesh axis runs over, the one named last changes fastest.
Arguments:
- hidden: bfloat16 [32, 1024, 16384], P('fsdp', 'cp'), may hold values from -6 to 6
- norm_gain: bfloat16 [16384], P('fsdp'), may hold values from 0.25 to 1.75
- query_weight: bfloat16 [16384, 256], P('fsdp'), may hold values from -0.0625 to 0.0625
- key_weight: bfloat16 [16384, 128], P('fsdp'), may hold values from -0.0625 to 0.0625
- value_weight: bfloat16 [16384, 128], P('fsdp'), may hold values from -0.046875 to 0.046875
- out_weight: bfloat16 [256, 16384], P(None, 'fsdp'), may hold values from -0.75 to 0.75
- doc_lengths: int32 [32, 4], P('fsdp'), may hold values from 1 to 512, 1024 in all within a row
Outputs:
- attention_out: bfloat16 [32, 1024, 16384], P('fsdp', 'cp')
Inputs may be any that keep to these rules, and one draw needn't show every extreme that they name: `doc_lengths`: each row holds the lengths of the 4 documents of one sequence in order; they sum to 1024 and the longest is exactly 512.
All inputs are finite; a program needn't handle non-finite values.
Results may differ from a plain program's by a relative error of at most 0.012.
Values may be sent and summed in bfloat16 or wider, within the bound.
A program may use at most 128 MiB of HBM per device.

v0:
```python
import math
import jax
import jax.numpy as jnp
from jax import lax
from jax.sharding import PartitionSpec as P

BLK = 128
EPSILON = 1e-05
THETA = 500000.0


def side_by_side(arrays, axis, dim, along):
    columns = [a.reshape(*a.shape[:along], -1) for a in arrays]
    both = jnp.concatenate(columns, axis=along)
    out, at, outs = (lax.all_gather(both, axis, axis=dim, tiled=True), 0, [])
    for a, column in zip(arrays, columns):
        section = out[..., at : at + column.shape[along]]
        outs.append(section.reshape(*section.shape[:along], *a.shape[along:]))
        at += column.shape[along]
    return tuple(outs)


def copy_for_each(array, axis):
    length = lax.axis_size(axis)
    return lax.all_to_all(
        jnp.broadcast_to(array[None], (length, *array.shape)), axis, 0, 0, tiled=True
    )


def laid_out(tiles, dim):
    tiles = jnp.moveaxis(tiles, 0, dim)
    shape = tiles.shape
    return tiles.reshape(*shape[:dim], shape[dim] * shape[dim + 1], *shape[dim + 2 :])


def gathered_copies(array, axis, dim):
    tiles = copy_for_each(array, axis)
    return laid_out(tiles, dim)


def side_by_side_2(arrays, axis, dim, along):
    ends, at = ([], 0)
    for a in arrays[:-1]:
        at += a.shape[along]
        ends.append(at)
    both = jnp.concatenate(arrays, axis=along)
    return tuple(jnp.split(gathered_copies(both, axis, dim), ends, axis=along))


def doc_tables(lengths, total):
    ends = jnp.cumsum(lengths)
    starts = ends - lengths
    places = jnp.arange(total, dtype=jnp.int32)
    after = (ends[None, :] <= places[:, None]).astype(jnp.int32)
    doc_ids = jnp.sum(after, axis=1)
    member = (doc_ids[:, None] == jnp.arange(lengths.shape[0], dtype=jnp.int32)[None, :]).astype(
        jnp.int32
    )
    offsets = places - jnp.sum(member * starts[None, :], axis=1)
    return (doc_ids, offsets)


def rotate(values, offsets):
    head_dim = values.shape[2]
    half = head_dim // 2
    rates = jnp.power(THETA, -2.0 * jnp.arange(half, dtype=jnp.float32) / head_dim)
    angles = offsets.astype(jnp.float32)[:, None] * rates[None, :]
    cosine = jnp.cos(angles)[:, None, :]
    sine = jnp.sin(angles)[:, None, :]
    first = values[:, :, :half]
    second = values[:, :, half:]
    return jnp.concatenate([first * cosine - second * sine, second * cosine + first * sine], axis=2)


def fold_panels(columns, pieces):
    gain_piece, query_piece, key_piece, value_piece = pieces
    normed = (columns * gain_piece.astype(jnp.float32)[None, :]).astype(jnp.bfloat16)
    return (
        jnp.dot(normed, query_piece, preferred_element_type=jnp.float32),
        jnp.dot(normed, key_piece, preferred_element_type=jnp.float32),
        jnp.dot(normed, value_piece, preferred_element_type=jnp.float32),
    )


def keep_same(operand):
    return operand


def attend_blocks(blocks, doc_ids, state, pieces):
    key_rows, value_rows = pieces
    count = key_rows.shape[0]
    tile_size = math.gcd(count, BLK)

    def one_tile(tile_index, inner):
        first = tile_index * tile_size
        key_tile = lax.dynamic_slice_in_dim(key_rows, tile_index * tile_size, tile_size, 0)
        value_tile = lax.dynamic_slice_in_dim(value_rows, tile_index * tile_size, tile_size, 0)
        key_places = first + jnp.arange(tile_size, dtype=jnp.int32)
        key_docs = lax.dynamic_slice_in_dim(doc_ids, first, tile_size, 0)
        updated = []
        for block, carried in zip(blocks, inner):
            queries, query_first = block
            length = queries.shape[1]
            query_docs = lax.dynamic_slice_in_dim(doc_ids, query_first, length, 0)
            query_places = query_first + jnp.arange(length, dtype=jnp.int32)
            live = jnp.logical_and(
                first <= query_first + length - 1, key_docs[tile_size - 1] >= query_docs[0]
            )

            def compute(operand):
                numer, denom = operand
                scores = jnp.einsum(
                    "hqd,kd->hqk", queries, key_tile, preferred_element_type=jnp.float32
                )
                allowed = jnp.logical_and(
                    query_docs[:, None] == key_docs[None, :],
                    key_places[None, :] <= query_places[:, None],
                )
                weights = jnp.where(allowed[None, :, :], jnp.exp(scores), jnp.float32(0.0))
                numer = numer + jnp.einsum(
                    "hqk,kd->hqd",
                    weights.astype(jnp.bfloat16),
                    value_tile,
                    preferred_element_type=jnp.float32,
                )
                return (numer, denom + jnp.sum(weights, axis=2))

            updated.append(lax.cond(live, compute, keep_same, carried))
        return tuple(updated)

    return lax.fori_loop(0, count // tile_size, one_tile, state)


def local(hidden, norm_gain, query_weight, key_weight, value_weight, out_weight, doc_lengths):
    rows = hidden.shape[1]
    head_dim = key_weight.shape[1]
    heads = query_weight.shape[1] // head_dim
    groups = lax.axis_size("cp")
    position = lax.axis_index("cp")
    doc_ids, offsets = doc_tables(doc_lengths[0], rows * groups)
    tokens = hidden[0].astype(jnp.float32)
    scaled = tokens * lax.rsqrt(jnp.mean(tokens * tokens, axis=1, keepdims=True) + EPSILON)
    query_raw, key_raw, value_raw = fold_panels(
        scaled, side_by_side((norm_gain, query_weight, key_weight, value_weight), "fsdp", 0, 1)
    )
    own_offsets = lax.dynamic_slice_in_dim(offsets, position * rows, rows, 0)
    queries = (
        rotate(query_raw.reshape(rows, heads, head_dim), own_offsets) * head_dim ** (-0.5)
    ).astype(jnp.bfloat16)
    queries = queries.transpose(1, 0, 2)
    key_rows = rotate(key_raw.reshape(rows, 1, head_dim), own_offsets)[:, 0, :].astype(jnp.bfloat16)
    value_rows = value_raw.astype(jnp.bfloat16)
    blocks = ((queries, position * rows),)
    start_state = tuple(
        (
            (
                jnp.zeros((heads, block[0].shape[1], head_dim), jnp.float32),
                jnp.zeros((heads, block[0].shape[1]), jnp.float32),
            )
            for block in blocks
        )
    )
    state = attend_blocks(
        blocks, doc_ids, start_state, side_by_side_2((key_rows, value_rows), "cp", 0, 1)
    )
    results = [
        (numer / denom[:, :, None])
        .astype(jnp.bfloat16)
        .transpose(1, 0, 2)
        .reshape(numer.shape[1], heads * head_dim)
        for numer, denom in state
    ]
    attended = results[0]
    mixed = jnp.dot(
        attended,
        lax.all_gather(out_weight, "fsdp", axis=1, tiled=True),
        preferred_element_type=jnp.float32,
    ).astype(jnp.bfloat16)
    return mixed[None, :, :]


def solution(mesh):
    in_specs = (
        P("fsdp", "cp", None),
        P("fsdp"),
        P("fsdp", None),
        P("fsdp", None),
        P("fsdp", None),
        P(None, "fsdp"),
        P("fsdp", None),
    )
    out_specs = P("fsdp", "cp", None)
    return jax.shard_map(local, mesh=mesh, in_specs=in_specs, out_specs=out_specs, check_vma=False)
```

profile of v0, /device:TPU:1, one launch (start us, length us, event | category | flops | bytes accessed | tf_op | source)
XLA Modules:
  0.0 229.7 jit_solution(12196940942636767293)
XLA Ops:
  6.5 0.8 reshape.223
  7.4 2.3 pad_maximum_fusion
  9.7 0.7 all-gather.5.cloned.1.call-update
  10.4 0.8 reduce-window.4
  11.4 0.7 fusion.48
  12.2 3.1 %fusion.12 = f32[128]{0:T(128)S(1)} fusion(bf16[1,128,16384]{2,1,0:T(8,128)(2,1)} %param.11), kind=kLoop, calls=%fused_computation.20 | loop fusion | flops 6291328 | bytes 4194816 | tf_op jit(solution)/shard_map/reduce_sum | solution.py:142
  15.3 0.2 multiply_cosine_fusion
  15.5 119.3 %all-gather.3.cloned.1.call-done = bf16[16384,513]{1,0:T(8,128)(2,1)} async-done(((bf16[512,513]{1,0:T(8,128)(2,1)}), bf16[16384,513]{1,0:T(8,128)(2,1)}) %all-gather.3.cloned.1.call-update) | async-done | bytes 16810000 | tf_op jit(solution)/shard_map/all_gather | solution.py:15
  134.9 3.0 %convert_reduce_fusion = f32[16384]{0:T(1024)S(1)} fusion(bf16[16384,513]{1,0:T(8,128)(2,1)} %all-gather.3.cloned.1.call-done), kind=kLoop, calls=%fused_computation.26 | loop fusion | flops 16384 | bytes 98304 | tf_op jit(solution)/shard_map/convert_element_type | solution.py:77
  137.9 8.3 %fusion.28 = f32[128,1,128]{0,2,1:T(8,128)S(1)} fusion(bf16[16384,513]{1,0:T(8,128)(2,1)} %all-gather.3.cloned.1.call-done, bf16[1,128,16384]{2,1,0:T(8,128)(2,1)} %param.11, f32[16384]{0:T(1024)S(1)} %convert_reduce_fusion, f32[128]{0:T(128)S(1)} %add_rsqrt_fusion), kind=kOutput, calls=%fused_computation.35 | convolution fusion | flops 545259520 | bytes 8520192 | tf_op jit(solution)/shard_map/dot_general | solution.py:80
  146.2 0.2 fusion.45
  146.5 7.2 %fusion.33 = bf16[128,128]{0,1:T(8,128)(2,1)S(1)} fusion(bf16[16384,513]{1,0:T(8,128)(2,1)} %all-gather.3.cloned.1.call-done, bf16[1,128,16384]{2,1,0:T(8,128)(2,1)S(1)} %copy-done, f32[16384]{0:T(1024)S(1)} %convert_reduce_fusion, f32[128]{0:T(128)S(1)} %add_rsqrt_fusion), kind=kOutput, calls=%fused_computation.36 | convolution fusion | flops 545275904 | bytes 8487424 | tf_op jit(solution)/shard_map/dot_general | solution.py:81
  153.8 0.8 broadcast_in_dim.23
  154.6 8.9 %all-to-all-start = ((bf16[8,128,256]{2,1,0:T(8,128)(2,1)}), bf16[8,128,256]{2,1,0:T(8,128)(2,1)S(1)}, u32[]{:S(2)}, u32[]{:S(2)}) async-start(bf16[8,128,256]{2,1,0:T(8,128)(2,1)} %broadcast_in_dim.23), calls=%async_computation | async-start | bytes 1048576 | tf_op jit(solution)/shard_map/all_to_all | solution.py:25
  163.5 9.9 %slice_bitcast_fusion = bf16[256,16384]{0,1:T(8,128)(2,1)} fusion(bf16[16384,513]{1,0:T(8,128)(2,1)} %all-gather.3.cloned.1.call-done), kind=kLoop, calls=%fused_computation.25 | loop fusion | bytes 16777216 | tf_op jit(solution)/shard_map/dot_general | solution.py:79
  173.4 12.0 %copy.21 = bf16[256,16384]{1,0:T(8,128)(2,1)} copy(bf16[256,16384]{0,1:T(8,128)(2,1)} %slice_bitcast_fusion) | data formatting | bytes 16777216 | tf_op jit(solution)/shard_map/dot_general | solution.py:79
  185.3 7.3 %fusion.18 = f32[128,2,128]{0,2,1:T(8,128)S(1)} fusion(bf16[2,128,16384]{2,1,0:T(8,128)(2,1)} %bitcast.68, bf16[1,128,16384]{2,1,0:T(8,128)(2,1)} %param.11, f32[16384]{0:T(1024)S(1)} %convert_reduce_fusion, f32[128]{0:T(128)S(1)} %add_rsqrt_fusion), kind=kOutput, calls=%fused_computation.28 | convolution fusion | flops 1082130432 | bytes 12780032 | tf_op jit(solution)/shard_map/dot_general | solution.py:79
  192.6 0.1 copy.22
  192.9 11.9 %while.17 = (s32[]{:T(128)}, f32[2,128,128]{2,1,0:T(8,128)S(1)}, f32[2,128]{1,0:T(2,128)S(1)}, s32[]{:T(128)}, s32[1024]{0:T(1024)S(1)}, /*index=5*/s32[128]{0:T...) while((s32[]{:T(128)}, f32[2,128,128]{2,1,0:T(8,128)S(1)}, ...), condition=%wide.region_8.9_spmd, body=%wide.region_4.8_spmd.sunk | while | flops 16957704 | bytes 567161 | solution.py:131
  193.0 0.6 slice.77
  194.2 0.6 conditional.2
  194.4 0.2 fusion.49
  194.6 0.2 convolution_add_fusion
  194.9 0.6 slice.77
  196.3 0.6 slice.77
  197.8 0.6 slice.77
  199.2 0.6 slice.77
  200.6 0.6 slice.77
  202.0 0.6 slice.77
  203.4 0.6 slice.77
  204.9 11.3 %all-gather.5.cloned.1.call-done = bf16[256,16384]{1,0:T(8,128)(2,1)} async-done(((bf16[256,512]{1,0:T(8,128)(2,1)}), bf16[256,16384]{1,0:T(8,128)(2,1)}) %all-gather.5.cloned.1.call-update) | async-done | bytes 8388624 | tf_op jit(solution)/shard_map/all_gather | solution.py:176
  216.2 6.7 %fusion.9 = bf16[1,128,16384]{2,1,0:T(8,128)(2,1)} fusion(bf16[128,256]{0,1:T(8,128)(2,1)S(1)} %bitcast.70, bf16[256,16384]{1,0:T(8,128)(2,1)} %all-gather.5.cloned.1.call-done), kind=kOutput, calls=%fused_computation.15 | convolution fusion | flops 1075838976 | bytes 12648448 | tf_op jit(solution)/shard_map/dot_general | solution.py:174
  (49 shorter events, 1.6 us)
Async XLA Ops:
  6.5 128.3 %all-gather.3.cloned.1.call-start = ((), (), s32[]{:S(2)}) async-start(), calls=%async_computation.1 | async-start | bytes 21626880 | tf_op jit(solution)/shard_map/all_gather | solution.py:15
  9.6 206.5 %all-gather.5.cloned.1.call-start = ((), (), s32[]{:S(2)}) async-start(), calls=%async_computation.2 | async-start | bytes 8650752 | tf_op jit(solution)/shard_map/all_gather | solution.py:176
  134.9 11.6 %copy-start = (bf16[1,128,16384]{2,1,0:T(8,128)(2,1)S(1)}, bf16[1,128,16384]{2,1,0:T(8,128)(2,1)}, u32[]{:S(2)}) copy-start(bf16[1,128,16384]{2,1,0:T(8,128)(2,1)} %param.11) | copy-start | bytes 12582916
  154.6 38.2 %all-to-all-start = ((bf16[8,128,256]{2,1,0:T(8,128)(2,1)}), bf16[8,128,256]{2,1,0:T(8,128)(2,1)S(1)}, u32[]{:S(2)}, u32[]{:S(2)}) async-start(bf16[8,128,256]{2,1,0:T(8,128)(2,1)} %broadcast_in_dim.23), calls=%async_computation | async-start | bytes 1048576 | tf_op jit(solution)/shard_map/all_to_all | solution.py:25
Sparse Core Ops, SparseCore 0:
  9.8 125.0 all-gather.2
  136.7 79.3 all-gather.4
where the time goes:
time: 230 us
  waiting for transfers between devices  131 us (57%)
  matrix products  29.8 us (13%)
  local copies, waits for them, and re-layouts  29.7 us (13%)
  between operations  13.6 us (6%)
  other arithmetic  10.7 us (5%)
  starting transfers between devices  8.9 us (4%)
  loops' own time  5.59 us (2%)
    all_gather x1, waiting for transfers between devices, side_by_side(): out, at, outs = (lax.all_gather(both, axis, axis=dim, tiled=True), 0, [])  119 us
    dot_general x2, local copies, waits for them, and re-layouts, fold_panels(): jnp.dot(normed, query_piece, preferred_element_type=jnp.float32)  21.9 us
    all_gather x1, waiting for transfers between devices, local(): lax.all_gather(out_weight, 'fsdp', axis=1, tiled=True)  11.3 us
    all_to_all x1, starting transfers between devices, copy_for_each(): lax.all_to_all(jnp.broadcast_to(array[None], (length, *array.shape)), axi...  8.86 us
    dot_general x1, matrix products, fold_panels(): jnp.dot(normed, key_piece, preferred_element_type=jnp.float32)  8.33 us
    dot_general x1, matrix products, fold_panels(): jnp.dot(normed, query_piece, preferred_element_type=jnp.float32)  7.26 us
    dot_general x1, matrix products, fold_panels(): jnp.dot(normed, value_piece, preferred_element_type=jnp.float32)  7.16 us
    dot_general x1, matrix products, local(): jnp.dot(attended, lax.all_gather(out_weight, 'fsdp', axis=1, tiled=True),...  6.69 us
  transfers between devices with their start and end apart: 3, of which 2 were waited for; matrix products, arithmetic and copies ran while one was open for 26% of the time, Pallas kernels for 0%

commit v1 on v0

--- a/solution.py
+++ b/solution.py
@@ -1,12 +1,22 @@
+import functools
 import math
 import jax
 import jax.numpy as jnp
 from jax import lax
 from jax.sharding import PartitionSpec as P
+from jax.lax import all_to_all, axis_size
 
 BLK = 128
 EPSILON = 1e-05
 THETA = 500000.0
+
+
+def serve_the_signs(tile_in, lane_axis):
+    oldest = jnp.stack([tile_in] * axis_size(lane_axis))
+    return jnp.concatenate(all_to_all(oldest, lane_axis, 0, 0), axis=1)
+
+
+_remake_panel = functools.partial(serve_the_signs, lane_axis="fsdp")
 
 
 def side_by_side(arrays, axis, dim, along):
@@ -171,11 +181,9 @@
         for numer, denom in state
     ]
     attended = results[0]
-    mixed = jnp.dot(
-        attended,
-        lax.all_gather(out_weight, "fsdp", axis=1, tiled=True),
-        preferred_element_type=jnp.float32,
-    ).astype(jnp.bfloat16)
+    mixed = jnp.dot(attended, _remake_panel(out_weight), preferred_element_type=jnp.float32).astype(
+        jnp.bfloat16
+    )
     return mixed[None, :, :]
 
 

time: 230 us -> 394 us (1.71)
  waiting for transfers between devices: 131 us -> 280 us
  starting transfers between devices: 8.9 us -> 18.5 us
  local copies, waits for them, and re-layouts: 29.7 us -> 33.8 us
    all_to_all x0 -> x1, waiting for transfers between devices: none -> 144 us  [serve_the_signs(): return jnp.concatenate(all_to_all(oldest, lane_axis, 0, 0), axis=1)]
    all_to_all x1, waiting for transfers between devices: 0.01 us -> 15.3 us  [copy_for_each(): lax.all_to_all(jnp.broadcast_to(array[None], (length, *array.shape)), axi...]
    all_gather x1 -> x0, waiting for transfers between devices: 11.3 us -> none  [local(): lax.all_gather(out_weight, 'fsdp', axis=1, tiled=True)]
    all_to_all x0 -> x1, starting transfers between devices: none -> 9.56 us  [serve_the_signs(): return jnp.concatenate(all_to_all(oldest, lane_axis, 0, 0), axis=1)]
    another operation x0 -> x1, local copies, waits for them, and re-layouts: none -> 4.27 us  [serve_the_signs(): oldest = jnp.stack([tile_in] * axis_size(lane_axis))]
  transfers between devices with their start and end apart: 3 -> 3, of which waited for: 2 -> 3; matrix products, arithmetic and copies ran while one was open for 26% -> 10% of each run, Pallas kernels for 0% -> 0%
where the time goes in v1:
time: 394 us; the launch traced here: 393 us
  waiting for transfers between devices  280 us (71%)
  local copies, waits for them, and re-layouts  33.8 us (9%)
  matrix products  31 us (8%)
  starting transfers between devices  18.5 us (5%)
  between operations  13.6 us (3%)
  other arithmetic  10.7 us (3%)
  loops' own time  5.5 us (1%)
    all_to_all x1, waiting for transfers between devices, serve_the_signs(): return jnp.concatenate(all_to_all(oldest, lane_axis, 0, 0), axis=1)  144 us
    all_gather x1, waiting for transfers between devices, side_by_side(): out, at, outs = (lax.all_gather(both, axis, axis=dim, tiled=True), 0, [])  120 us
    dot_general x2, local copies, waits for them, and re-layouts, fold_panels(): jnp.dot(normed, query_piece, preferred_element_type=jnp.float32)  21.8 us
    all_to_all x1, waiting for transfers between devices, copy_for_each(): lax.all_to_all(jnp.broadcast_to(array[None], (length, *array.shape)), axi...  15.3 us
    all_to_all x1, starting transfers between devices, serve_the_signs(): return jnp.concatenate(all_to_all(oldest, lane_axis, 0, 0), axis=1)  9.56 us
    all_to_all x1, starting transfers between devices, copy_for_each(): lax.all_to_all(jnp.broadcast_to(array[None], (length, *array.shape)), axi...  8.97 us
    dot_general x1, matrix products, fold_panels(): jnp.dot(normed, key_piece, preferred_element_type=jnp.float32)  8.26 us
    dot_general x1, matrix products, local(): jnp.dot(attended, _remake_panel(out_weight), preferred_element_type=jnp.f...  8.23 us
  transfers between devices with their start and end apart: 3, of which 3 were waited for; matrix products, arithmetic and copies ran while one was open for 10% of the time, Pallas kernels for 0%

profile of v1, /device:TPU:1, one launch (start us, length us, event | category | flops | bytes accessed | tf_op | source)
XLA Modules:
  0.0 393.0 jit_solution(14187622417109735787)
XLA Ops:
  6.5 0.8 reshape.233
  7.4 2.3 pad_maximum_fusion
  9.6 0.8 reduce-window.4
  10.6 0.7 fusion.48
  11.4 3.1 fusion.12
  14.5 120.4 %all-gather.2.cloned.1.call-done = bf16[16384,513]{1,0:T(8,128)(2,1)} async-done(((bf16[512,513]{1,0:T(8,128)(2,1)}), bf16[16384,513]{1,0:T(8,128)(2,1)}) %all-gather.2.cloned.1.call-update) | async-done | bytes 16810000 | tf_op jit(solution)/shard_map/all_gather | solution.py:25
  134.9 3.0 convert_reduce_fusion
  137.9 8.3 %fusion.28 = f32[128,1,128]{0,2,1:T(8,128)S(1)} fusion(bf16[16384,513]{1,0:T(8,128)(2,1)} %all-gather.2.cloned.1.call-done, bf16[1,128,16384]{2,1,0:T(8,128)(2,1)} %param.11, f32[16384]{0:T(1024)S(1)} %convert_reduce_fusion, f32[128]{0:T(128)S(1)} %add_rsqrt_fusion), kind=kOutput, calls=%fused_computation.35 | convolution fusion | flops 545259520 | bytes 8520192 | tf_op jit(solution)/shard_map/dot_general | solution.py:90
  146.2 0.2 fusion.45
  146.4 7.0 %fusion.33 = bf16[128,128]{0,1:T(8,128)(2,1)S(1)} fusion(bf16[16384,513]{1,0:T(8,128)(2,1)} %all-gather.2.cloned.1.call-done, bf16[1,128,16384]{2,1,0:T(8,128)(2,1)S(1)} %copy-done, f32[16384]{0:T(1024)S(1)} %convert_reduce_fusion, f32[128]{0:T(128)S(1)} %add_rsqrt_fusion), kind=kOutput, calls=%fused_computation.36 | convolution fusion | flops 545275904 | bytes 8487424 | tf_op jit(solution)/shard_map/dot_general | solution.py:91
  153.6 0.8 broadcast_in_dim.23
  154.4 9.0 %all-to-all-start = ((bf16[8,128,256]{2,1,0:T(8,128)(2,1)}), bf16[8,128,256]{2,1,0:T(8,128)(2,1)S(1)}, u32[]{:S(2)}, u32[]{:S(2)}) async-start(bf16[8,128,256]{2,1,0:T(8,128)(2,1)} %broadcast_in_dim.23), calls=%async_computation | async-start | bytes 1048576 | tf_op jit(solution)/shard_map/all_to_all | solution.py:35
  163.5 15.3 %all-to-all-done = bf16[8,128,256]{2,1,0:T(8,128)(2,1)S(1)} async-done(((bf16[8,128,256]{2,1,0:T(8,128)(2,1)}), bf16[8,128,256]{2,1,0:T(8,128)(2,1)S(1)}, u32[]{:S(2)}, u32[]{:S(2)}) %all-to-all-start) | async-done | bytes 524320 | tf_op jit(solution)/shard_map/all_to_all | solution.py:35
  178.8 4.3 %stack.2 = bf16[32,256,512]{1,2,0:T(8,128)(2,1)} broadcast(bf16[256,512]{0,1:T(8,128)(2,1)S(1)} %copy.25), dimensions={1,2} | broadcast | bytes 8650752 | tf_op jit(solution)/shard_map/stack | solution.py:15
  183.1 9.6 %all-to-all-start.1 = ((bf16[32,256,512]{1,2,0:T(8,128)(2,1)}), bf16[32,256,512]{1,2,0:T(8,128)(2,1)}, u32[]{:S(2)}, u32[]{:S(2)}) async-start(bf16[32,256,512]{1,2,0:T(8,128)(2,1)} %stack.2), calls=%async_computation.1 | async-start | bytes 16777216 | tf_op jit(solution)/shard_map/all_to_all | solution.py:16
  192.9 9.8 %slice_bitcast_fusion = bf16[256,16384]{0,1:T(8,128)(2,1)} fusion(bf16[16384,513]{1,0:T(8,128)(2,1)} %all-gather.2.cloned.1.call-done), kind=kLoop, calls=%fused_computation.25 | loop fusion | bytes 16777216 | tf_op jit(solution)/shard_map/dot_general | solution.py:89
  202.7 12.0 %copy.22 = bf16[256,16384]{1,0:T(8,128)(2,1)} copy(bf16[256,16384]{0,1:T(8,128)(2,1)} %slice_bitcast_fusion) | data formatting | bytes 16777216 | tf_op jit(solution)/shard_map/dot_general | solution.py:89
  214.7 7.0 %fusion.18 = f32[128,2,128]{0,2,1:T(8,128)S(1)} fusion(bf16[2,128,16384]{2,1,0:T(8,128)(2,1)} %bitcast.71, bf16[1,128,16384]{2,1,0:T(8,128)(2,1)} %param.11, f32[16384]{0:T(1024)S(1)} %convert_reduce_fusion, f32[128]{0:T(128)S(1)} %add_rsqrt_fusion), kind=kOutput, calls=%fused_computation.28 | convolution fusion | flops 1082130432 | bytes 12780032 | tf_op jit(solution)/shard_map/dot_general | solution.py:89
  222.0 11.6 %while.17 = (s32[]{:T(128)}, f32[2,128,128]{2,1,0:T(8,128)S(1)}, f32[2,128]{1,0:T(2,128)S(1)}, s32[]{:T(128)}, s32[1024]{0:T(1024)S(1)}, /*index=5*/s32[128]{0:T...) while((s32[]{:T(128)}, f32[2,128,128]{2,1,0:T(8,128)S(1)}, ...), condition=%wide.region_8.9_spmd, body=%wide.region_4.8_spmd.sunk | while | flops 16957704 | bytes 567153 | solution.py:141
  222.1 0.6 slice.77
  223.3 0.6 conditional.2
  223.5 0.2 fusion.49
  223.7 0.2 convolution_add_fusion
  224.0 0.6 slice.77
  225.4 0.6 slice.77
  226.8 0.6 slice.77
  228.1 0.6 slice.77
  229.5 0.6 slice.77
  230.9 0.6 slice.77
  232.3 0.6 slice.77
  233.7 144.2 %all-to-all-done.1 = bf16[32,256,512]{1,2,0:T(8,128)(2,1)} async-done(((bf16[32,256,512]{1,2,0:T(8,128)(2,1)}), bf16[32,256,512]{1,2,0:T(8,128)(2,1)}, u32[]{:S(2)}, u32[]{:S(2)}) %all-to-all-start.1) | async-done | bytes 8388640 | tf_op jit(solution)/shard_map/all_to_all | solution.py:16
  377.9 8.2 %fusion.9 = bf16[1,128,16384]{2,1,0:T(8,128)(2,1)} fusion(bf16[128,256]{0,1:T(8,128)(2,1)S(1)} %bitcast.73, bf16[256,16384]{0,1:T(8,128)(2,1)} %bitcast.20), kind=kOutput, calls=%fused_computation.15 | convolution fusion | flops 1075838976 | bytes 12648448 | tf_op jit(solution)/shard_map/dot_general | solution.py:184
  (52 shorter events, 2.0 us)
Async XLA Ops:
  6.5 128.3 %all-gather.2.cloned.1.call-start = ((), (), s32[]{:S(2)}) async-start(), calls=%async_computation.2 | async-start | bytes 21626880 | tf_op jit(solution)/shard_map/all_gather | solution.py:25
  134.9 11.5 %copy-start = (bf16[1,128,16384]{2,1,0:T(8,128)(2,1)S(1)}, bf16[1,128,16384]{2,1,0:T(8,128)(2,1)}, u32[]{:S(2)}) copy-start(bf16[1,128,16384]{2,1,0:T(8,128)(2,1)} %param.11) | copy-start | bytes 12582916
  146.2 17.2 %copy-start.1 = (bf16[256,512]{1,0:T(8,128)(2,1)S(1)}, bf16[256,512]{1,0:T(8,128)(2,1)}, u32[]{:S(2)}) copy-start(bf16[256,512]{1,0:T(8,128)(2,1)} %param.16) | copy-start | bytes 786436
  154.4 24.4 %all-to-all-start = ((bf16[8,128,256]{2,1,0:T(8,128)(2,1)}), bf16[8,128,256]{2,1,0:T(8,128)(2,1)S(1)}, u32[]{:S(2)}, u32[]{:S(2)}) async-start(bf16[8,128,256]{2,1,0:T(8,128)(2,1)} %broadcast_in_dim.23), calls=%async_computation | async-start | bytes 1048576 | tf_op jit(solution)/shard_map/all_to_all | solution.py:35
  183.1 194.8 %all-to-all-start.1 = ((bf16[32,256,512]{1,2,0:T(8,128)(2,1)}), bf16[32,256,512]{1,2,0:T(8,128)(2,1)}, u32[]{:S(2)}, u32[]{:S(2)}) async-start(bf16[32,256,512]{1,2,0:T(8,128)(2,1)} %stack.2), calls=%async_computation.1 | async-start | bytes 16777216 | tf_op jit(solution)/shard_map/all_to_all | solution.py:16
Sparse Core Ops, SparseCore 0:
  9.8 125.0 all-gather.1
